TPU v7x, 32 devices: a whole 2x2x4 slice. The times are simulated.
32 devices in a mesh: grp: 2 (over core), tile: 16 (over z, y, x).
Axes of the slice: x: 2, y: 2, z: 4, core: 2. Of those that a mesh axis runs over, the one named last changes fastest.
Arguments:
- basis: bfloat16 [32, 5, 64, 16, 128], P(None, None, 'tile'), may hold values from -18 to 18
- snapshots: bfloat16 [2, 4, 64, 16, 128], P('grp', None, 'tile'), may hold values from -1.5 to 1.5
- coupling: float32 [5, 5], replicated, may hold values from -2.5 to 2.5
Outputs:
- new_vector: float32 [2, 5, 64, 16, 128], P('grp', None, 'tile')
- coefficients: float32 [2, 32], P('grp')
- norms: float32 [2], P('grp')
All inputs are finite; a program needn't handle non-finite values.
Results may differ from a plain program's by a relative error of at most 0.0003.
Values may be sent and summed in bfloat16 or wider, within the bound.
A program may use at most 64 MiB of HBM per device.

v0:
```python
import jax
import jax.numpy as jnp
from jax import lax
from jax.sharding import PartitionSpec as P

viscosity = 0.5
time_step = 0.3


def extended_2(cells, sides, width):
    for axis, dim in sides:
        count = lax.axis_size(axis)
        head = lax.slice_in_dim(cells, 0, width, axis=dim)
        tail = lax.slice_in_dim(cells, cells.shape[dim] - width, cells.shape[dim], axis=dim)
        cells = jnp.concatenate(
            [
                lax.ppermute(tail, axis, [(i, (i + 1) % count) for i in range(count)]),
                cells,
                lax.ppermute(head, axis, [((i + 1) % count, i) for i in range(count)]),
            ],
            axis=dim,
        )
    return cells


def tendency(extended, base, coupling):
    center = extended[:, 1:-1]
    slope_x = 0.5 * (extended[:, 2:] - extended[:, :-2])
    walled = jnp.pad(center, ((0, 0), (0, 0), (1, 1), (0, 0)))
    upper_y = walled[:, :, 2:]
    lower_y = walled[:, :, :-2]
    slope_y = 0.5 * (upper_y - lower_y)
    upper_z = jnp.roll(center, -1, axis=3)
    lower_z = jnp.roll(center, 1, axis=3)
    slope_z = 0.5 * (upper_z - lower_z)
    laplace = (
        extended[:, 2:] + extended[:, :-2] + upper_y + lower_y + upper_z + lower_z - 6.0 * center
    )
    advect = base[0] * slope_x + base[1] * slope_y + base[2] * slope_z
    coupled = jnp.einsum("kj,jxyz->kxyz", coupling, center, precision=lax.Precision.HIGHEST)
    return viscosity * laplace - advect - base[3] * coupled


def advance_margin(state, rimmed, coupling):
    extended = extended_2(state, (("tile", 1),), 3)
    first = extended[:, 1:-1] + time_step * tendency(extended, rimmed, coupling)
    second = 0.75 * extended[:, 2:-2] + 0.25 * (
        first[:, 1:-1] + time_step * tendency(first, rimmed[:, 1:-1], coupling)
    )
    return extended[:, 3:-3] / 3.0 + 2.0 / 3.0 * (
        second[:, 1:-1] + time_step * tendency(second, rimmed[:, 2:-2], coupling)
    )


def project(flat_basis, vector):
    return jnp.dot(
        flat_basis, vector, precision=lax.Precision.HIGHEST, preferred_element_type=jnp.float32
    )


def expand(weights, flat_basis):
    return jnp.dot(
        weights, flat_basis, precision=lax.Precision.HIGHEST, preferred_element_type=jnp.float32
    )


def on_device(basis, snapshots, coupling):
    krylov = basis.shape[0]
    groups = lax.axis_size("grp")
    tiles = lax.axis_size("tile")
    position = krylov - groups + lax.axis_index("grp")
    state = lax.dynamic_index_in_dim(basis, position, 0, keepdims=False).astype(jnp.float32)
    history = lax.all_gather(snapshots, "grp", axis=0, tiled=True)
    rim_history = extended_2(history, (("tile", 2),), 2)
    for step_index in range(history.shape[0]):
        state = advance_margin(state, rim_history[step_index].astype(jnp.float32), coupling)
    flat_basis = basis.reshape(krylov, -1)
    vector = state.reshape(-1)
    count = jnp.float32(vector.shape[0] * tiles)
    first_coef = lax.psum(project(flat_basis, vector), "tile") / count
    first_left = vector - expand(first_coef, flat_basis)
    second_coef = lax.psum(project(flat_basis, first_left), "tile") / count
    second_left = first_left - expand(second_coef, flat_basis)
    square = lax.psum(jnp.sum(second_left * second_left), "tile") / count
    norm_value = jnp.sqrt(square)
    result = (second_left / norm_value).reshape((1,) + state.shape)
    return (result, (first_coef + second_coef).reshape(1, krylov), norm_value.reshape(1))


def solution(mesh):
    placed = (P(None, None, "tile", None, None), P("grp", None, "tile", None, None), P())
    return jax.shard_map(
        on_device,
        mesh=mesh,
        in_specs=placed,
        out_specs=(P("grp", None, "tile", None, None), P("grp", None), P("grp")),
        check_vma=False,
    )
```

profile of v0, /device:TPU:0, one launch (start us, length us, event | category | flops | bytes accessed | tf_op | source)
XLA Modules:
  0.0 171.1 jit_solution(726461644226535034)
XLA Ops:
  0.6 0.0 copy-start
  0.6 2.2 %all_gather.3 = bf16[2,4,4,16,128]{4,3,2,1,0:T(8,128)(2,1)S(1)} all-gather(bf16[1,4,4,16,128]{4,3,2,1,0:T(8,128)(2,1)} %param.4), channel_id=1, replica_groups=mesh['grp'=2,'tile'=16] {'grp'}, dimensions={0}, use_global_device_ids=true | all-gather | bytes 196608 | tf_op jit(solution)/shard_map/all_gather | solution.py:73
  2.9 2.9 %collective-permute-start.2 = (bf16[2,4,2,16,128]{4,3,2,1,0:T(8,128)(2,1)S(1)}, bf16[2,4,2,16,128]{4,3,2,1,0:T(8,128)(2,1)S(1)}, u32[]{:S(2)}, u32[]{:S(2)}) collective-permute-start(bf16[2,4,2,16,128]{4,3,2,1,0:T(8,128)(2,1)S(1)} %get-tuple-element.62), channel_id=1, source_target_pairs={{0,1},{1,2},{2,3},{3,4},{4,5},{5,6},{6,7},{7,8},{8,9},{9,10},{10,1... | collective-permute-start | bytes 196616 | tf_op jit(solution)/shard_map/ppermute | solution.py:17
  5.8 0.9 constant_dynamic-slice_fusion
  6.7 0.1 fusion.50
  6.8 1.5 collective-permute-start
  8.3 4.1 %collective-permute-start.1 = (f32[5,3,16,128]{3,0,2,1:T(8,128)S(1)}, f32[5,3,16,128]{3,0,2,1:T(8,128)S(1)}, u32[]{:S(2)}, u32[]{:S(2)}) collective-permute-start(f32[5,3,16,128]{3,0,2,1:T(8,128)S(1)} %get-tuple-element.60), channel_id=1, source_target_pairs={{1,0},{2,1},{3,2},{4,3},{5,4},{6,5},{7,6},{8,7},{9,8},{10,9},{11,1... | collective-permute-start | bytes 368648 | tf_op jit(solution)/shard_map/ppermute | solution.py:19
  12.5 0.5 collective-permute-start.3
  12.9 0.0 collective-permute-done.2
  13.0 7.1 %collective-permute-done.3 = bf16[2,4,2,16,128]{4,3,2,1,0:T(8,128)(2,1)S(1)} collective-permute-done((bf16[2,4,2,16,128]{4,3,2,1,0:T(8,128)(2,1)S(1)}, bf16[2,4,2,16,128]{4,3,2,1,0:T(8,128)(2,1)S(1)}, u32[]{:S(2)}, u32[]{:S(2)}) %collective-permute-start.3) | collective-permute-done | bytes 65568 | tf_op jit(solution)/shard_map/ppermute | solution.py:19
  20.1 0.1 fusion.58
  20.3 0.0 collective-permute-done.1
  20.3 0.1 pad_maximum_fusion
  20.4 0.2 fusion.87
  20.6 0.2 fusion.88
  20.9 1.1 fusion.18
  21.9 0.2 fusion.91
  22.1 0.2 fusion.92
  22.3 0.9 fusion.48
  23.2 0.1 fusion.95
  23.3 0.1 fusion.96
  23.5 0.6 fusion.37
  24.2 1.5 collective-permute-start.4
  25.7 4.1 %collective-permute-start.5 = (f32[5,3,16,128]{3,0,2,1:T(8,128)S(1)}, f32[5,3,16,128]{3,0,2,1:T(8,128)S(1)}, u32[]{:S(2)}, u32[]{:S(2)}) collective-permute-start(f32[5,3,16,128]{3,0,2,1:T(8,128)S(1)} %get-tuple-element.46), channel_id=1, source_target_pairs={{1,0},{2,1},{3,2},{4,3},{5,4},{6,5},{7,6},{8,7},{9,8},{10,9},{11,1... | collective-permute-start | bytes 368648 | tf_op jit(solution)/shard_map/ppermute | solution.py:19
  29.9 3.9 %collective-permute-done.4 = f32[5,3,16,128]{3,0,2,1:T(8,128)S(1)} collective-permute-done((f32[5,3,16,128]{3,0,2,1:T(8,128)S(1)}, f32[5,3,16,128]{3,0,2,1:T(8,128)S(1)}, u32[]{:S(2)}, u32[]{:S(2)}) %collective-permute-start.4) | collective-permute-done | bytes 122912 | tf_op jit(solution)/shard_map/ppermute | solution.py:17
  33.8 2.9 %collective-permute-done.5 = f32[5,3,16,128]{3,0,2,1:T(8,128)S(1)} collective-permute-done((f32[5,3,16,128]{3,0,2,1:T(8,128)S(1)}, f32[5,3,16,128]{3,0,2,1:T(8,128)S(1)}, u32[]{:S(2)}, u32[]{:S(2)}) %collective-permute-start.5) | collective-permute-done | bytes 122912 | tf_op jit(solution)/shard_map/ppermute | solution.py:19
  36.7 0.1 pad_maximum_fusion.1
  36.7 0.2 fusion.85
  36.9 0.2 fusion.86
  37.2 1.1 fusion.14
  38.2 0.2 fusion.89
  38.4 0.2 fusion.90
  38.6 0.9 fusion.47
  39.5 0.0 copy-start.1
  39.5 0.1 fusion.93
  39.7 0.1 fusion.94
  39.8 0.6 fusion.40
  40.5 0.8 copy-done.1
  41.3 3.5 %fusion.41 = f32[32]{0:T(128)S(1)} fusion(bf16[32,5,4,16,128]{4,3,2,1,0:T(8,128)(2,1)S(1)} %copy-done.1, f32[5,4,16,128,1]{3,0,2,1,4:T(8,128)S(1)} %bitcast.180), kind=kOutput, calls=%fused_computation.47 | convolution fusion | flops 15728640 | bytes 2785408 | tf_op jit(solution)/shard_map/dot_general | solution.py:56
  44.8 39.2 %psum.21 = f32[32]{0:T(128)S(1)} all-reduce(f32[32]{0:T(128)S(1)} %fusion.41), channel_id=1, replica_groups=mesh['grp'=2,'tile'=16] {'tile'}, use_global_device_ids=true, to_apply=%region_0.1 | all-reduce | flops 32 | bytes 256 | tf_op jit(solution)/shard_map/psum | solution.py:80
  84.0 2.2 %fusion.4 = f32[1,40960]{1,0:T(1,128)S(1)} fusion(bf16[4,8,320,128]{3,2,1,0:T(8,128)(2,1)S(1)} %bitcast.177, f32[32]{0:T(128)S(1)} %psum.21), kind=kOutput, calls=%fused_computation.4 | convolution fusion | flops 15728672 | bytes 2785408 | tf_op jit(solution)/shard_map/dot_general | solution.py:62
  86.2 3.1 %fusion.44 = f32[32]{0:T(128)S(1)} fusion(f32[40960,1]{0,1:T(1,128)S(1)} %bitcast.183, bf16[4,8,320,128]{3,2,1,0:T(8,128)(2,1)S(1)} %bitcast.178), kind=kOutput, calls=%fused_computation.48 | convolution fusion | flops 15728640 | bytes 2785408 | tf_op jit(solution)/shard_map/dot_general | solution.py:56
  89.4 36.6 %psum.22 = f32[32]{0:T(128)S(1)} all-reduce(f32[32]{0:T(128)S(1)} %fusion.44), channel_id=1, replica_groups=mesh['grp'=2,'tile'=16] {'tile'}, use_global_device_ids=true, to_apply=%region_1.2 | all-reduce | flops 32 | bytes 256 | tf_op jit(solution)/shard_map/psum | solution.py:82
  126.0 0.5 add_bitcast_fusion
  126.5 2.2 %fusion = f32[1,40960]{1,0:T(1,128)S(1)} fusion(bf16[4,8,320,128]{3,2,1,0:T(8,128)(2,1)S(1)} %bitcast.179, f32[32]{0:T(128)S(1)} %psum.22), kind=kOutput, calls=%fused_computation | convolution fusion | flops 15728672 | bytes 2785408 | tf_op jit(solution)/shard_map/dot_general | solution.py:62
  128.7 0.6 multiply_reduce_fusion
  129.4 39.2 %psum.23 = f32[]{:T(128)} all-reduce(f32[]{:T(128)} %get-tuple-element.3), channel_id=1, replica_groups=mesh['grp'=2,'tile'=16] {'tile'}, use_global_device_ids=true, to_apply=%region_3.4 | all-reduce | flops 1 | bytes 8 | tf_op jit(solution)/shard_map/psum | solution.py:84
  169.2 0.7 broadcast_divide_fusion
  (22 shorter events, 0.4 us)
Async XLA Ops:
  0.6 20.2 %copy-start = (f32[5,5]{1,0:T(8,128)S(1)}, f32[5,5]{1,0:T(8,128)}, u32[]{:S(2)}) copy-start(f32[5,5]{1,0:T(8,128)} %param.5) | copy-start | bytes 304
  2.9 10.0 %collective-permute-start.2 = (bf16[2,4,2,16,128]{4,3,2,1,0:T(8,128)(2,1)S(1)}, bf16[2,4,2,16,128]{4,3,2,1,0:T(8,128)(2,1)S(1)}, u32[]{:S(2)}, u32[]{:S(2)}) collective-permute-start(bf16[2,4,2,16,128]{4,3,2,1,0:T(8,128)(2,1)S(1)} %get-tuple-element.62), channel_id=1, source_target_pairs={{0,1},{1,2},{2,3},{3,4},{4,5},{5,6},{6,7},{7,8},{8,9},{9,10},{10,1... | collective-permute-start | bytes 196616 | tf_op jit(solution)/shard_map/ppermute | solution.py:17
  6.8 13.5 %collective-permute-start = (f32[5,3,16,128]{3,0,2,1:T(8,128)S(1)}, f32[5,3,16,128]{3,0,2,1:T(8,128)S(1)}, u32[]{:S(2)}, u32[]{:S(2)}) collective-permute-start(f32[5,3,16,128]{3,0,2,1:T(8,128)S(1)} %get-tuple-element.59), channel_id=1, source_target_pairs={{0,1},{1,2},{2,3},{3,4},{4,5},{5,6},{6,7},{7,8},{8,9},{9,10},{10,1... | collective-permute-start | bytes 368648 | tf_op jit(solution)/shard_map/ppermute | solution.py:17
  8.3 12.0 %collective-permute-start.1 = (f32[5,3,16,128]{3,0,2,1:T(8,128)S(1)}, f32[5,3,16,128]{3,0,2,1:T(8,128)S(1)}, u32[]{:S(2)}, u32[]{:S(2)}) collective-permute-start(f32[5,3,16,128]{3,0,2,1:T(8,128)S(1)} %get-tuple-element.60), channel_id=1, source_target_pairs={{1,0},{2,1},{3,2},{4,3},{5,4},{6,5},{7,6},{8,7},{9,8},{10,9},{11,1... | collective-permute-start | bytes 368648 | tf_op jit(solution)/shard_map/ppermute | solution.py:19
  12.5 7.6 %collective-permute-start.3 = (bf16[2,4,2,16,128]{4,3,2,1,0:T(8,128)(2,1)S(1)}, bf16[2,4,2,16,128]{4,3,2,1,0:T(8,128)(2,1)S(1)}, u32[]{:S(2)}, u32[]{:S(2)}) collective-permute-start(bf16[2,4,2,16,128]{4,3,2,1,0:T(8,128)(2,1)S(1)} %get-tuple-element.61), channel_id=1, source_target_pairs={{1,0},{2,1},{3,2},{4,3},{5,4},{6,5},{7,6},{8,7},{9,8},{10,9},{11,1... | collective-permute-start | bytes 196616 | tf_op jit(solution)/shard_map/ppermute | solution.py:19
  24.2 9.6 %collective-permute-start.4 = (f32[5,3,16,128]{3,0,2,1:T(8,128)S(1)}, f32[5,3,16,128]{3,0,2,1:T(8,128)S(1)}, u32[]{:S(2)}, u32[]{:S(2)}) collective-permute-start(f32[5,3,16,128]{3,0,2,1:T(8,128)S(1)} %get-tuple-element.45), channel_id=1, source_target_pairs={{0,1},{1,2},{2,3},{3,4},{4,5},{5,6},{6,7},{7,8},{8,9},{9,10},{10,1... | collective-permute-start | bytes 368648 | tf_op jit(solution)/shard_map/ppermute | solution.py:17
  25.7 10.9 %collective-permute-start.5 = (f32[5,3,16,128]{3,0,2,1:T(8,128)S(1)}, f32[5,3,16,128]{3,0,2,1:T(8,128)S(1)}, u32[]{:S(2)}, u32[]{:S(2)}) collective-permute-start(f32[5,3,16,128]{3,0,2,1:T(8,128)S(1)} %get-tuple-element.46), channel_id=1, source_target_pairs={{1,0},{2,1},{3,2},{4,3},{5,4},{6,5},{7,6},{8,7},{9,8},{10,9},{11,1... | collective-permute-start | bytes 368648 | tf_op jit(solution)/shard_map/ppermute | solution.py:19
  39.5 1.7 %copy-start.1 = (bf16[32,5,4,16,128]{4,3,2,1,0:T(8,128)(2,1)S(1)}, bf16[32,5,4,16,128]{4,3,2,1,0:T(8,128)(2,1)}, u32[]{:S(2)}) copy-start(bf16[32,5,4,16,128]{4,3,2,1,0:T(8,128)(2,1)} %param.3) | copy-start | bytes 7864324
where the time goes:
time: 171 us
  blocking collectives  117 us (68%)
  matrix products  16.2 us (9%)
  starting transfers between devices  14.7 us (9%)
  waiting for transfers between devices  13.9 us (8%)
  local copies, waits for them, and re-layouts  4.06 us (2%)
  between operations  2.73 us (2%)
  other arithmetic  2.24 us (1%)
    psum x1, blocking collectives, on_device(): first_coef = lax.psum(project(flat_basis, vector), 'tile') / count  39.2 us
    psum x1, blocking collectives, on_device(): square = lax.psum(jnp.sum(second_left * second_left), 'tile') / count  39.2 us
    psum x1, blocking collectives, on_device(): second_coef = lax.psum(project(flat_basis, first_left), 'tile') / count  36.6 us
    ppermute x3, waiting for transfers between devices, extended_2(): lax.ppermute(head, axis, [((i + 1) % count, i) for i in range(count)])  10 us
    ppermute x3, starting transfers between devices, extended_2(): lax.ppermute(head, axis, [((i + 1) % count, i) for i in range(count)])  8.72 us
    dot_general x2, matrix products, project(): jnp.dot(flat_basis, vector, precision=lax.Precision.HIGHEST, preferred_el...  6.68 us
    ppermute x3, starting transfers between devices, extended_2(): lax.ppermute(tail, axis, [(i, (i + 1) % count) for i in range(count)])  5.97 us
    dot_general x6, matrix products, tendency(): jnp.einsum('kj,jxyz->kxyz', coupling, center, precision=lax.Precision.HIG...  5.05 us
  transfers between devices with their start and end apart: 6, of which 3 were waited for; matrix products, arithmetic and copies ran while one was open for 1% of the time, Pallas kernels for 0%

commit v1 on v0

v1 whole, which is shorter than its diff:
```python
import functools

import jax
import jax.numpy as jnp
from jax import lax
from jax.experimental import pallas as pl
from jax.experimental.pallas import tpu as pltpu
from jax.sharding import PartitionSpec as P

viscosity = 0.5
time_step = 0.3
f32 = jnp.float32
bf16 = jnp.bfloat16
MESH = pl.DeviceIdType.MESH
HIGHEST = lax.Precision.HIGHEST


def spans(slab, rim):
    found = {}
    reach = -(-rim // slab)
    for d in range(1, reach + 1):
        width = min(slab, rim - (d - 1) * slab)
        found[-d] = (slab - width, slab)
        found[d] = (0, width)
    return found


def stage(src, old, dst, snap, step, coupling, lo, hi, keep, gain):
    rows, lanes = src.shape[2], src.shape[3]
    row = lax.broadcasted_iota(jnp.int32, (rows, lanes), 0)
    first = row == 0
    last = row == rows - 1
    step_gain = time_step * gain
    mix = [[coupling[k, j] for j in range(5)] for k in range(5)]

    def body(i, carry):
        p = lo + i
        base = [snap[step, n, p].astype(f32) for n in range(4)]
        half = [(0.5 * step_gain) * base[n] for n in range(3)]
        edge = viscosity * step_gain
        x_up, x_low = edge - half[0], edge + half[0]
        y_up = jnp.where(last, 0.0, edge - half[1])
        y_low = jnp.where(first, 0.0, edge + half[1])
        z_up, z_low = edge - half[2], edge + half[2]
        pull = step_gain * base[3]
        center = [src[k, p] for k in range(5)]
        own = gain - 6.0 * viscosity * step_gain
        for k in range(5):
            q = center[k]
            coupled = mix[k][0] * center[0]
            for j in range(1, 5):
                coupled = coupled + mix[k][j] * center[j]
            total = own * q - pull * coupled
            total = total + (x_up * src[k, p + 1] + x_low * src[k, p - 1])
            total = total + (y_up * pltpu.roll(q, rows - 1, 0) + y_low * pltpu.roll(q, 1, 0))
            total = total + (z_up * pltpu.roll(q, lanes - 1, 1) + z_low * pltpu.roll(q, 1, 1))
            if keep:
                total = total + keep * old[k, p]
            dst[k, p] = total
        return carry

    lax.fori_loop(0, hi - lo, body, 0)


def kernel(
    groups, tiles, coupling, basis, snapshots,
    out, coef_out, norm_out,
    held, start, snap, state, one, two, cross, rows_k, spread, left,
    gram_send, gram_all, coef_send, coef_all, norm_send, norm_all,
    load_sem, start_send, start_recv, snap_send, snap_recv,
    gram_ssem, gram_rsem, coef_ssem, coef_rsem, norm_ssem, norm_rsem,
):
    g = lax.axis_index("grp")
    t = lax.axis_index("tile")
    krylov, parts, slab, ny, nz = basis.shape
    local = snapshots.shape[0]
    steps = local * groups
    rim = 3 * steps
    planes = slab + 2 * rim
    near = spans(slab, rim)
    offsets = sorted(near)
    position = krylov - groups + g

    def at(group, offset):
        return {"grp": group, "tile": lax.rem(t + (offset % tiles), tiles)}

    barrier = pltpu.get_barrier_semaphore()

    def greet(r, carry):
        pl.semaphore_signal(barrier, inc=1, device_id=at(g, 0) | {"tile": lax.rem(t + r, tiles)}, device_id_type=MESH)
        return carry

    lax.fori_loop(1, tiles, greet, 0)
    for other in range(1, groups):
        for d in [0] + offsets:
            pl.semaphore_signal(
                barrier, inc=1, device_id=at(lax.rem(g + other, groups), d), device_id_type=MESH
            )

    chunk = 8 if krylov % 8 == 0 else 1
    loads = []
    own = pltpu.make_async_copy(basis.at[position], start.at[:, pl.ds(rim, slab)], load_sem.at[0])
    own.start()
    for n in range(krylov // chunk):
        part = pl.ds(n * chunk, chunk)
        copy = pltpu.make_async_copy(basis.at[part], held.at[part], load_sem.at[1 + n])
        copy.start()
        loads.append(copy)

    pl.semaphore_wait(barrier, tiles - 1 + (groups - 1) * (1 + len(offsets)))

    def target(d, first, last):
        return pl.ds(rim + d * slab + first, last - first)

    start_copies = []
    for n, d in enumerate(offsets):
        first, last = near[d]
        start_copies.append(
            pltpu.make_async_remote_copy(
                src_ref=basis.at[position, :, pl.ds(first, last - first)],
                dst_ref=start.at[:, target(d, first, last)],
                send_sem=start_send.at[n],
                recv_sem=start_recv.at[n],
                device_id=at(g, -d),
                device_id_type=MESH,
            )
        )

    def snap_copy(s, n, d, other):
        first, last = (0, slab) if d == 0 else spans(slab, rim - 3 * s - 1)[d]
        return pltpu.make_async_remote_copy(
            src_ref=snapshots.at[s % local, :, pl.ds(first, last - first)],
            dst_ref=snap.at[s, :, target(d, first, last)],
            send_sem=snap_send.at[s % local, other, n],
            recv_sem=snap_recv.at[s, n],
            device_id=at(lax.rem(g + other, groups), -d),
            device_id_type=MESH,
        )

    def local_snap(s):
        return pltpu.make_async_copy(
            snapshots.at[s % local], snap.at[s, :, pl.ds(rim, slab)], load_sem.at[1 + krylov // chunk + s % local]
        )

    def snap_offsets(s):
        inside = spans(slab, rim - 3 * s - 1)
        return [(n, d) for n, d in enumerate([0] + offsets) if d == 0 or d in inside]

    for copy in start_copies:
        copy.start()
    for s in range(steps):
        @pl.when(g == s // local)
        def _():
            local_snap(s).start()
            for n, d in snap_offsets(s):
                for other in range(groups):
                    if d or other:
                        snap_copy(s, n, d, other).start()

    for copy in loads:
        copy.wait()
    size = krylov * ny
    wide = jnp.concatenate(
        [held[:, c, x].reshape(size, nz) for c in range(parts) for x in range(slab)], axis=1
    )
    cross[...] = lax.dot_general(
        wide, wide, (((1,), (1,)), ((), ())), preferred_element_type=f32
    )
    line = lax.broadcasted_iota(jnp.int32, (size, size), 0)
    column = lax.broadcasted_iota(jnp.int32, (size, size), 1)
    kept = jnp.where(lax.rem(line, ny) == lax.rem(column, ny), cross[...], 0.0)
    kept = jnp.sum(kept.reshape(krylov, ny, size), axis=1)
    pick = (
        lax.broadcasted_iota(jnp.int32, (size, krylov), 0) // ny
        == lax.broadcasted_iota(jnp.int32, (size, krylov), 1)
    ).astype(f32)
    gram_send[...] = jnp.dot(kept, pick, precision=HIGHEST, preferred_element_type=f32)

    def share(send, everyone, ssem, rsem):
        def copy(r):
            return pltpu.make_async_remote_copy(
                src_ref=send,
                dst_ref=everyone.at[t],
                send_sem=ssem.at[r],
                recv_sem=rsem.at[r],
                device_id={"grp": g, "tile": lax.rem(t + r, tiles)},
                device_id_type=MESH,
            )

        def begin():
            lax.fori_loop(1, tiles, lambda r, c: (copy(r).start(), c)[1], 0)
            everyone[t] = send[...]

        def arrive():
            def one_wait(r, c):
                pltpu.make_async_remote_copy(
                    src_ref=send,
                    dst_ref=everyone.at[lax.rem(t - r + tiles, tiles)],
                    send_sem=ssem.at[r],
                    recv_sem=rsem.at[r],
                    device_id={"grp": g, "tile": lax.rem(t + r, tiles)},
                    device_id_type=MESH,
                ).wait_recv()
                return c
            lax.fori_loop(1, tiles, one_wait, 0)

        def drain():
            lax.fori_loop(1, tiles, lambda r, c: (copy(r).wait_send(), c)[1], 0)

        return begin, arrive, drain

    gram_begin, gram_arrive, gram_drain = share(gram_send, gram_all, gram_ssem, gram_rsem)
    coef_begin, coef_arrive, coef_drain = share(coef_send, coef_all, coef_ssem, coef_rsem)
    norm_begin, norm_arrive, norm_drain = share(norm_send, norm_all, norm_ssem, norm_rsem)
    gram_begin()

    own.wait()
    for n, d in enumerate(offsets):
        first, last = near[d]
        pltpu.make_async_remote_copy(
            src_ref=basis.at[position, :, pl.ds(first, last - first)],
            dst_ref=start.at[:, target(d, first, last)],
            send_sem=start_send.at[n],
            recv_sem=start_recv.at[n],
            device_id=at(g, -d),
            device_id_type=MESH,
        ).wait_recv()
    for s in range(steps):
        @pl.when(g == s // local)
        def _():
            local_snap(s).wait()
        if groups > 1:
            @pl.when(g != s // local)
            def _():
                snap_copy(s, 0, 0, 1).wait_recv()
        for n, d in snap_offsets(s):
            if d:
                snap_copy(s, n, d, 1 % groups).wait_recv()

    def widen(p, carry):
        for k in range(parts):
            state[k, p] = start[k, p].astype(f32)
        return carry

    lax.fori_loop(0, planes, widen, 0)
    lo, hi = 0, planes
    for s in range(steps):
        stage(state, state, one, snap, s, coupling, lo + 1, hi - 1, 0.0, 1.0)
        stage(one, state, two, snap, s, coupling, lo + 2, hi - 2, 0.75, 0.25)
        stage(two, state, state, snap, s, coupling, lo + 3, hi - 3, 1.0 / 3.0, 2.0 / 3.0)
        lo, hi = lo + 3, hi - 3

    count = f32(parts * slab * ny * nz * tiles)

    def project(k, carry):
        total = jnp.zeros((ny, nz), f32)
        for c in range(parts):
            for x in range(slab):
                total = total + held[k, c, x].astype(f32) * state[c, rim + x]
        rows_k[pl.ds(k, 1), :] = jnp.sum(total, axis=0, keepdims=True)
        return carry

    lax.fori_loop(0, krylov, project, 0)
    ones = jnp.ones((8, nz), f32)
    inner = lax.dot_general(
        ones, rows_k[...], (((1,), (1,)), ((), ())), precision=HIGHEST, preferred_element_type=f32
    )
    coef_send[...] = inner[0:1]
    coef_begin()
    gram_arrive()
    gram = jnp.sum(gram_all[...], axis=0) / count
    coef_arrive()
    first_coef = jnp.sum(coef_all[...], axis=0) / count
    first_rows = jnp.broadcast_to(first_coef, (8, krylov))
    second_rows = first_rows - jnp.dot(first_rows, gram, precision=HIGHEST, preferred_element_type=f32)
    both = first_rows + second_rows
    coef_out[...] = both[0:1]
    for k in range(krylov):
        spread[k] = jnp.broadcast_to(both[:, k : k + 1], (8, nz))

    def subtract(x, total):
        for c in range(parts):
            value = state[c, rim + x]
            removed = jnp.zeros((ny // 8, 8, nz), f32)
            for k in range(krylov):
                removed = removed + spread[k][None] * held[k, c, x].astype(f32).reshape(ny // 8, 8, nz)
            value = value - removed.reshape(ny, nz)
            left[c, x] = value
            total = total + value * value
        return total

    total = lax.fori_loop(0, slab, subtract, jnp.zeros((ny, nz), f32))
    norm_send[...] = jnp.sum(total, axis=0, keepdims=True)
    norm_begin()
    for copy in start_copies:
        copy.wait_send()
    for s in range(steps):
        @pl.when(g == s // local)
        def _():
            for n, d in snap_offsets(s):
                for other in range(groups):
                    if d or other:
                        snap_copy(s, n, d, other).wait_send()
    gram_drain()
    coef_drain()
    norm_arrive()
    square = jnp.sum(jnp.sum(norm_all[...], axis=0), axis=1, keepdims=True) / count
    norm = jnp.sqrt(square)
    norm_out[...] = jnp.broadcast_to(norm, norm_out.shape)
    inverse = jnp.broadcast_to(1.0 / norm, (ny, nz))
    for c in range(parts):
        for x in range(slab):
            out[0, c, x] = left[c, x] * inverse
    norm_drain()


def on_device(groups, tiles, basis, snapshots, coupling):
    krylov, parts, slab, ny, nz = basis.shape
    local, fields = snapshots.shape[:2]
    steps = local * groups
    rim = 3 * steps
    planes = slab + 2 * rim
    count = len(spans(slab, rim))
    dma = pltpu.SemaphoreType.DMA
    field = pltpu.VMEM((parts, planes, ny, nz), f32)
    whole = pl.BlockSpec(memory_space=pltpu.VMEM)
    new_vector, coefs, norms = pl.pallas_call(
        functools.partial(kernel, groups, tiles),
        name="propagate",
        out_shape=(
            jax.ShapeDtypeStruct((1, parts, slab, ny, nz), f32),
            jax.ShapeDtypeStruct((1, krylov), f32),
            jax.ShapeDtypeStruct((1, nz), f32),
        ),
        in_specs=[
            pl.BlockSpec(memory_space=pltpu.SMEM),
            pl.BlockSpec(memory_space=pl.ANY),
            pl.BlockSpec(memory_space=pl.ANY),
        ],
        out_specs=(whole, whole, whole),
        scratch_shapes=[
            pltpu.VMEM(basis.shape, bf16),
            pltpu.VMEM((parts, planes, ny, nz), bf16),
            pltpu.VMEM((steps, fields, planes, ny, nz), bf16),
            field,
            field,
            field,
            pltpu.VMEM((krylov * ny, krylov * ny), f32),
            pltpu.VMEM((krylov, nz), f32),
            pltpu.VMEM((krylov, 8, nz), f32),
            pltpu.VMEM((parts, slab, ny, nz), f32),
            pltpu.VMEM((krylov, krylov), f32),
            pltpu.VMEM((tiles, krylov, krylov), f32),
            pltpu.VMEM((1, krylov), f32),
            pltpu.VMEM((tiles, 1, krylov), f32),
            pltpu.VMEM((1, nz), f32),
            pltpu.VMEM((tiles, 1, nz), f32),
            dma((1 + krylov + local,)),
            dma((count,)),
            dma((count,)),
            dma((local, groups, count + 1)),
            dma((steps, count + 1)),
            dma((tiles,)),
            dma((tiles,)),
            dma((tiles,)),
            dma((tiles,)),
            dma((tiles,)),
            dma((tiles,)),
        ],
        compiler_params=pltpu.CompilerParams(
            collective_id=0, has_side_effects=True, vmem_limit_bytes=50 * 2**20
        ),
    )(coupling, basis, snapshots)
    return new_vector, coefs, norms[0, :1]


def solution(mesh):
    placed = (P(None, None, "tile", None, None), P("grp", None, "tile", None, None), P())
    return jax.shard_map(
        functools.partial(on_device, mesh.shape["grp"], mesh.shape["tile"]),
        mesh=mesh,
        in_specs=placed,
        out_specs=(P("grp", None, "tile", None, None), P("grp", None), P("grp")),
        check_vma=False,
    )
```

time: 171 us -> 43.3 us (0.25)
  blocking collectives: 117 us -> 0 us
  Pallas kernels: 0 us -> 36.9 us
  matrix products: 16.2 us -> 0 us
  starting transfers between devices: 14.7 us -> 0 us
  waiting for transfers between devices: 13.9 us -> 0 us
  other arithmetic: 2.24 us -> 0 us
    psum x3 -> x0, blocking collectives: 115 us -> none  [the longest x1 39.2 us: on_device(): first_coef = lax.psum(project(flat_basis, vector), 'tile') / count]
    pallas_call x0 -> x1, Pallas kernels: none -> 36.9 us  [on_device(): pl.pallas_call(functools.partial(kernel, groups, tiles), name='propagate'...]
    dot_general x10 -> x0, matrix products: 16.2 us -> none  [the longest x2 6.68 us: project(): jnp.dot(flat_basis, vector, precision=lax.Precision.HIGHEST, preferred_el...]
    ppermute x6 -> x0, starting transfers between devices: 14.7 us -> none  [the longest x3 8.72 us: extended_2(): lax.ppermute(head, axis, [((i + 1) % count, i) for i in range(count)])]
    ppermute x6 -> x0, waiting for transfers between devices: 13.9 us -> none  [the longest x3 10 us: extended_2(): lax.ppermute(head, axis, [((i + 1) % count, i) for i in range(count)])]
    unnamed x6 -> x8, local copies, waits for them, and re-layouts: 0.81 us -> 4.44 us
    slice x21 -> x0, local copies, waits for them, and re-layouts: 2.31 us -> none  [the longest x12 2.08 us: tendency(): upper_z = jnp.roll(center, -1, axis=3)]
    all_gather x1 -> x0, blocking collectives: 2.25 us -> none  [on_device(): history = lax.all_gather(snapshots, 'grp', axis=0, tiled=True)]
  transfers between devices with their start and end apart: 6 -> 0, of which waited for: 3 -> 0; matrix products, arithmetic and copies ran while one was open for 1% -> 0% of each run, Pallas kernels for 0% -> 0%
where the time goes in v1:
time: 43.3 us; the launch traced here: 43.1 us
  Pallas kernels  36.9 us (85%)
  local copies, waits for them, and re-layouts  4.44 us (10%)
  between operations  1.81 us (4%)
    pallas_call x1, Pallas kernels, on_device(): pl.pallas_call(functools.partial(kernel, groups, tiles), name='propagate'...  36.9 us
    unnamed x8, local copies, waits for them, and re-layouts  4.44 us

profile of v1, /device:TPU:0, one launch (start us, length us, event | category | flops | bytes accessed | tf_op | source)
XLA Modules:
  0.0 43.1 jit_solution(3763089907883281453)
XLA Ops:
  0.6 0.0 copy-start
  0.6 1.7 %copy-done = bf16[32,5,4,16,128]{4,3,2,1,0:T(8,128)(2,1)S(1)} copy-done((bf16[32,5,4,16,128]{4,3,2,1,0:T(8,128)(2,1)S(1)}, bf16[32,5,4,16,128]{4,3,2,1,0:T(8,128)(2,1)}, u32[]{:S(2)}) %copy-start) | copy-done | bytes 2621464
  2.4 0.0 copy-start.1
  2.4 0.8 %copy-done.1 = bf16[1,4,4,16,128]{4,3,2,1,0:T(8,128)(2,1)S(1)} copy-done((bf16[1,4,4,16,128]{4,3,2,1,0:T(8,128)(2,1)S(1)}, bf16[1,4,4,16,128]{4,3,2,1,0:T(8,128)(2,1)}, u32[]{:S(2)}) %copy-start.1) | copy-done | bytes 65560
  3.2 0.0 copy-start.2
  3.2 0.7 %copy-done.2 = f32[5,5]{1,0:T(8,128)S(1)} copy-done((f32[5,5]{1,0:T(8,128)S(1)}, f32[5,5]{1,0:T(8,128)}, u32[]{:S(2)}) %copy-start.2) | copy-done | bytes 124
  3.9 36.9 %propagate.1 = (f32[1,5,4,16,128]{4,3,2,1,0:T(8,128)S(1)}, f32[1,32]{1,0:T(1,128)S(1)}, f32[1,128]{1,0:T(1,128)S(1)}) custom-call(f32[5,5]{1,0:T(8,128)S(1)} %copy-done.2, bf16[32,5,4,16,128]{4,3,2,1,0:T(8,128)(2,1)S(1)} %copy-done, bf16[1,4,4,16,128]{4,3,2,1,0:T(8,128)(2,1)S(1)} %copy-done.1), custom_call_target="tpu_custom_call" | custom-call | tf_op jit(solution)/shard_map/propagate/pallas_call | solution.py:327
  40.8 0.7 %copy.9 = f32[1,5,4,16,128]{4,3,2,1,0:T(8,128)} copy(f32[1,5,4,16,128]{4,3,2,1,0:T(8,128)S(1)} %get-tuple-element.12) | data formatting | bytes 327680
  41.4 0.5 %copy.10 = f32[1,32]{1,0:T(1,128)} copy(f32[1,32]{1,0:T(1,128)S(1)} %get-tuple-element.13) | data formatting | bytes 256
Async XLA Ops:
  0.6 1.7 %copy-start = (bf16[32,5,4,16,128]{4,3,2,1,0:T(8,128)(2,1)S(1)}, bf16[32,5,4,16,128]{4,3,2,1,0:T(8,128)(2,1)}, u32[]{:S(2)}) copy-start(bf16[32,5,4,16,128]{4,3,2,1,0:T(8,128)(2,1)} %basis.1) | copy-start | bytes 7864324
  2.4 0.8 %copy-start.1 = (bf16[1,4,4,16,128]{4,3,2,1,0:T(8,128)(2,1)S(1)}, bf16[1,4,4,16,128]{4,3,2,1,0:T(8,128)(2,1)}, u32[]{:S(2)}) copy-start(bf16[1,4,4,16,128]{4,3,2,1,0:T(8,128)(2,1)} %snapshots.1) | copy-start | bytes 196612
  3.2 0.7 %copy-start.2 = (f32[5,5]{1,0:T(8,128)S(1)}, f32[5,5]{1,0:T(8,128)}, u32[]{:S(2)}) copy-start(f32[5,5]{1,0:T(8,128)} %coupling.1) | copy-start | bytes 304

commit v2 on v1

--- a/solution.py
+++ b/solution.py
@@ -59,13 +59,13 @@
             dst[k, p] = total
         return carry
 
-    lax.fori_loop(0, hi - lo, body, 0)
+    lax.fori_loop(0, hi - lo, body, 0, unroll=2)
 
 
 def kernel(
     groups, tiles, coupling, basis, snapshots,
-    out, coef_out, norm_out,
-    held, start, snap, state, one, two, cross, rows_k, spread, left,
+    left, coef_out, square_out,
+    held, start, snap, state, one, two, cross, rows_k, spread,
     gram_send, gram_all, coef_send, coef_all, norm_send, norm_all,
     load_sem, start_send, start_recv, snap_send, snap_recv,
     gram_ssem, gram_rsem, coef_ssem, coef_rsem, norm_ssem, norm_rsem,
@@ -92,10 +92,9 @@
 
     lax.fori_loop(1, tiles, greet, 0)
     for other in range(1, groups):
-        for d in [0] + offsets:
-            pl.semaphore_signal(
-                barrier, inc=1, device_id=at(lax.rem(g + other, groups), d), device_id_type=MESH
-            )
+        pl.semaphore_signal(
+            barrier, inc=1, device_id=at(lax.rem(g + other, groups), 0), device_id_type=MESH
+        )
 
     chunk = 8 if krylov % 8 == 0 else 1
     loads = []
@@ -106,56 +105,6 @@
         copy = pltpu.make_async_copy(basis.at[part], held.at[part], load_sem.at[1 + n])
         copy.start()
         loads.append(copy)
-
-    pl.semaphore_wait(barrier, tiles - 1 + (groups - 1) * (1 + len(offsets)))
-
-    def target(d, first, last):
-        return pl.ds(rim + d * slab + first, last - first)
-
-    start_copies = []
-    for n, d in enumerate(offsets):
-        first, last = near[d]
-        start_copies.append(
-            pltpu.make_async_remote_copy(
-                src_ref=basis.at[position, :, pl.ds(first, last - first)],
-                dst_ref=start.at[:, target(d, first, last)],
-                send_sem=start_send.at[n],
-                recv_sem=start_recv.at[n],
-                device_id=at(g, -d),
-                device_id_type=MESH,
-            )
-        )
-
-    def snap_copy(s, n, d, other):
-        first, last = (0, slab) if d == 0 else spans(slab, rim - 3 * s - 1)[d]
-        return pltpu.make_async_remote_copy(
-            src_ref=snapshots.at[s % local, :, pl.ds(first, last - first)],
-            dst_ref=snap.at[s, :, target(d, first, last)],
-            send_sem=snap_send.at[s % local, other, n],
-            recv_sem=snap_recv.at[s, n],
-            device_id=at(lax.rem(g + other, groups), -d),
-            device_id_type=MESH,
-        )
-
-    def local_snap(s):
-        return pltpu.make_async_copy(
-            snapshots.at[s % local], snap.at[s, :, pl.ds(rim, slab)], load_sem.at[1 + krylov // chunk + s % local]
-        )
-
-    def snap_offsets(s):
-        inside = spans(slab, rim - 3 * s - 1)
-        return [(n, d) for n, d in enumerate([0] + offsets) if d == 0 or d in inside]
-
-    for copy in start_copies:
-        copy.start()
-    for s in range(steps):
-        @pl.when(g == s // local)
-        def _():
-            local_snap(s).start()
-            for n, d in snap_offsets(s):
-                for other in range(groups):
-                    if d or other:
-                        snap_copy(s, n, d, other).start()
 
     for copy in loads:
         copy.wait()
@@ -176,6 +125,92 @@
     ).astype(f32)
     gram_send[...] = jnp.dot(kept, pick, precision=HIGHEST, preferred_element_type=f32)
 
+    pl.semaphore_wait(barrier, tiles - 1 + groups - 1)
+
+    def target(d, first, last):
+        return pl.ds(rim + d * slab + first, last - first)
+
+    start_copies = []
+    for n, d in enumerate(offsets):
+        first, last = near[d]
+        start_copies.append(
+            pltpu.make_async_remote_copy(
+                src_ref=basis.at[position, :, pl.ds(first, last - first)],
+                dst_ref=start.at[:, target(d, first, last)],
+                send_sem=start_send.at[n],
+                recv_sem=start_recv.at[n],
+                device_id=at(g, -d),
+                device_id_type=MESH,
+            )
+        )
+
+    def snap_copy(s, n, d, other):
+        first, last = (0, slab) if d == 0 else spans(slab, rim - 3 * s - 1)[d]
+        return pltpu.make_async_remote_copy(
+            src_ref=snapshots.at[s % local, :, pl.ds(first, last - first)],
+            dst_ref=snap.at[s, :, target(d, first, last)],
+            send_sem=snap_send.at[s % local, other, n],
+            recv_sem=snap_recv.at[s, n],
+            device_id=at(lax.rem(g + other, groups), -d),
+            device_id_type=MESH,
+        )
+
+    def local_snap(s):
+        return pltpu.make_async_copy(
+            snapshots.at[s % local], snap.at[s, :, pl.ds(rim, slab)], load_sem.at[1 + krylov // chunk + s % local]
+        )
+
+    def snap_offsets(s):
+        inside = spans(slab, rim - 3 * s - 1)
+        return [(n, d) for n, d in enumerate([0] + offsets) if d == 0 or d in inside]
+
+    def send_snap(s):
+        @pl.when(g == s // local)
+        def _():
+            local_snap(s).start()
+            for n, d in snap_offsets(s):
+                for other in range(1 if d else groups):
+                    if d or other:
+                        snap_copy(s, n, d, other).start()
+
+    def relay_copy(s, n, d, other):
+        first, last = spans(slab, rim - 3 * s - 1)[d]
+        cells = snap.at[s, :, target(d, first, last)]
+        return pltpu.make_async_remote_copy(
+            src_ref=cells,
+            dst_ref=cells,
+            send_sem=snap_send.at[s % local, other, n],
+            recv_sem=snap_recv.at[s, n],
+            device_id=at(lax.rem(g + other, groups), 0),
+            device_id_type=MESH,
+        )
+
+    def relay(s):
+        @pl.when(g == s // local)
+        def _():
+            for n, d in snap_offsets(s):
+                if d:
+                    snap_copy(s, n, d, 0).wait_recv()
+                    for other in range(1, groups):
+                        relay_copy(s, n, d, other).start()
+            local_snap(s).wait()
+
+    def receive(s):
+        if groups > 1:
+            @pl.when(g != s // local)
+            def _():
+                snap_copy(s, 0, 0, 1).wait_recv()
+                for n, d in snap_offsets(s):
+                    if d:
+                        relay_copy(s, n, d, 1).wait_recv()
+
+    for s in range(local):
+        send_snap(s)
+    for copy in start_copies:
+        copy.start()
+    for s in range(local, steps):
+        send_snap(s)
+
     def share(send, everyone, ssem, rsem):
         def copy(r):
             return pltpu.make_async_remote_copy(
@@ -214,28 +249,10 @@
     norm_begin, norm_arrive, norm_drain = share(norm_send, norm_all, norm_ssem, norm_rsem)
     gram_begin()
 
+    relay(0)
     own.wait()
-    for n, d in enumerate(offsets):
-        first, last = near[d]
-        pltpu.make_async_remote_copy(
-            src_ref=basis.at[position, :, pl.ds(first, last - first)],
-            dst_ref=start.at[:, target(d, first, last)],
-            send_sem=start_send.at[n],
-            recv_sem=start_recv.at[n],
-            device_id=at(g, -d),
-            device_id_type=MESH,
-        ).wait_recv()
-    for s in range(steps):
-        @pl.when(g == s // local)
-        def _():
-            local_snap(s).wait()
-        if groups > 1:
-            @pl.when(g != s // local)
-            def _():
-                snap_copy(s, 0, 0, 1).wait_recv()
-        for n, d in snap_offsets(s):
-            if d:
-                snap_copy(s, n, d, 1 % groups).wait_recv()
+    for copy in start_copies:
+        copy.wait_recv()
 
     def widen(p, carry):
         for k in range(parts):
@@ -245,7 +262,11 @@
     lax.fori_loop(0, planes, widen, 0)
     lo, hi = 0, planes
     for s in range(steps):
+        receive(s)
         stage(state, state, one, snap, s, coupling, lo + 1, hi - 1, 0.0, 1.0)
+        if s == 0:
+            for later in range(1, steps):
+                relay(later)
         stage(one, state, two, snap, s, coupling, lo + 2, hi - 2, 0.75, 0.25)
         stage(two, state, state, snap, s, coupling, lo + 3, hi - 3, 1.0 / 3.0, 2.0 / 3.0)
         lo, hi = lo + 3, hi - 3
@@ -260,7 +281,7 @@
         rows_k[pl.ds(k, 1), :] = jnp.sum(total, axis=0, keepdims=True)
         return carry
 
-    lax.fori_loop(0, krylov, project, 0)
+    lax.fori_loop(0, krylov, project, 0, unroll=4)
     ones = jnp.ones((8, nz), f32)
     inner = lax.dot_general(
         ones, rows_k[...], (((1,), (1,)), ((), ())), precision=HIGHEST, preferred_element_type=f32
@@ -285,7 +306,7 @@
             for k in range(krylov):
                 removed = removed + spread[k][None] * held[k, c, x].astype(f32).reshape(ny // 8, 8, nz)
             value = value - removed.reshape(ny, nz)
-            left[c, x] = value
+            left[0, c, x] = value
             total = total + value * value
         return total
 
@@ -299,19 +320,26 @@
         def _():
             for n, d in snap_offsets(s):
                 for other in range(groups):
-                    if d or other:
+                    if d and other:
+                        relay_copy(s, n, d, other).wait_send()
+                    elif d or other:
                         snap_copy(s, n, d, other).wait_send()
     gram_drain()
     coef_drain()
     norm_arrive()
     square = jnp.sum(jnp.sum(norm_all[...], axis=0), axis=1, keepdims=True) / count
-    norm = jnp.sqrt(square)
-    norm_out[...] = jnp.broadcast_to(norm, norm_out.shape)
-    inverse = jnp.broadcast_to(1.0 / norm, (ny, nz))
-    for c in range(parts):
-        for x in range(slab):
-            out[0, c, x] = left[c, x] * inverse
+    square_out[...] = jnp.broadcast_to(square, square_out.shape)
     norm_drain()
+
+
+def finish(left, coefs, square, out, coef_out, norm_out):
+    norm = jnp.sqrt(square[...])
+    norm_out[...] = norm
+    coef_out[...] = coefs[...]
+    inverse = jnp.broadcast_to(1.0 / norm, left.shape[3:])
+    for c in range(left.shape[1]):
+        for x in range(left.shape[2]):
+            out[0, c, x] = left[0, c, x] * inverse
 
 
 def on_device(groups, tiles, basis, snapshots, coupling):
@@ -324,7 +352,7 @@
     dma = pltpu.SemaphoreType.DMA
     field = pltpu.VMEM((parts, planes, ny, nz), f32)
     whole = pl.BlockSpec(memory_space=pltpu.VMEM)
-    new_vector, coefs, norms = pl.pallas_call(
+    results = pl.pallas_call(
         functools.partial(kernel, groups, tiles),
         name="propagate",
         out_shape=(
@@ -348,7 +376,6 @@
             pltpu.VMEM((krylov * ny, krylov * ny), f32),
             pltpu.VMEM((krylov, nz), f32),
             pltpu.VMEM((krylov, 8, nz), f32),
-            pltpu.VMEM((parts, slab, ny, nz), f32),
             pltpu.VMEM((krylov, krylov), f32),
             pltpu.VMEM((tiles, krylov, krylov), f32),
             pltpu.VMEM((1, krylov), f32),
@@ -368,9 +395,16 @@
             dma((tiles,)),
         ],
         compiler_params=pltpu.CompilerParams(
-            collective_id=0, has_side_effects=True, vmem_limit_bytes=50 * 2**20
+            collective_id=0, has_side_effects=True, vmem_limit_bytes=67043328
         ),
     )(coupling, basis, snapshots)
+    new_vector, coefs, norms = pl.pallas_call(
+        finish,
+        name="finish",
+        out_shape=tuple(jax.ShapeDtypeStruct(a.shape, f32) for a in results),
+        in_specs=[whole] * 3,
+        out_specs=(whole, whole, whole),
+    )(*results)
     return new_vector, coefs, norms[0, :1]
 
 

time: 43.3 us -> 36.4 us (0.84)
  local copies, waits for them, and re-layouts: 4.44 us -> 0 us
  Pallas kernels: 36.9 us -> 35.5 us
  between operations: 1.81 us -> 0.64 us
    unnamed x8 -> x0, local copies, waits for them, and re-layouts: 4.44 us -> none
    pallas_call x1, Pallas kernels: 36.9 us -> 33.9 us  [on_device(): pl.pallas_call(functools.partial(kernel, groups, tiles), name='propagate'...]
    pallas_call x0 -> x1, Pallas kernels: none -> 1.62 us  [on_device(): pl.pallas_call(finish, name='finish', out_shape=tuple((jax.ShapeDtypeStru...]
where the time goes in v2:
time: 36.4 us; the launch traced here: 36.2 us
  Pallas kernels  35.5 us (98%)
  between operations  0.64 us (2%)
    pallas_call x1, Pallas kernels, on_device(): pl.pallas_call(functools.partial(kernel, groups, tiles), name='propagate'...  33.9 us
    pallas_call x1, Pallas kernels, on_device(): pl.pallas_call(finish, name='finish', out_shape=tuple((jax.ShapeDtypeStru...  1.62 us

profile of v2, /device:TPU:0, one launch (start us, length us, event | category | flops | bytes accessed | tf_op | source)
XLA Modules:
  0.0 36.2 jit_solution(16630265640124034326)
XLA Ops:
  0.6 33.9 %propagate.1 = (f32[1,5,4,16,128]{4,3,2,1,0:T(8,128)}, f32[1,32]{1,0:T(1,128)}, f32[1,128]{1,0:T(1,128)}) custom-call(f32[5,5]{1,0:T(8,128)} %coupling.1, bf16[32,5,4,16,128]{4,3,2,1,0:T(8,128)(2,1)} %basis.1, bf16[1,4,4,16,128]{4,3,2,1,0:T(8,128)(2,1)} %snapshots.1), custom_call_target="tpu_custom_call" | custom-call | tf_op jit(solution)/shard_map/propagate/pallas_call | solution.py:355
  34.5 1.6 %finish.1 = (f32[1,5,4,16,128]{4,3,2,1,0:T(8,128)}, f32[1,32]{1,0:T(1,128)}, f32[1,128]{1,0:T(1,128)}) custom-call(f32[1,5,4,16,128]{4,3,2,1,0:T(8,128)} %get-tuple-element.9.left, f32[1,32]{1,0:T(1,128)} %get-tuple-element.10.coefs, f32[1,128]{1,0:T(1,128)} %get-tuple-element.11.square), custom_call_target="tpu_custom_call" | custom-call | tf_op jit(solution)/shard_map/finish/pallas_call | solution.py:401

commit v3 on v2

--- a/solution.py
+++ b/solution.py
@@ -23,6 +23,11 @@
         found[-d] = (slab - width, slab)
         found[d] = (0, width)
     return found
+
+
+def gram_blocks(krylov, lanes):
+    blocks = max(lanes // krylov, 1)
+    return (blocks, krylov // blocks) if krylov % (8 * blocks) == 0 else (1, krylov)
 
 
 def stage(src, old, dst, snap, step, coupling, lo, hi, keep, gain):
@@ -59,7 +64,7 @@
             dst[k, p] = total
         return carry
 
-    lax.fori_loop(0, hi - lo, body, 0, unroll=2)
+    lax.fori_loop(0, hi - lo, body, 0, unroll=4)
 
 
 def kernel(
@@ -123,7 +128,11 @@
         lax.broadcasted_iota(jnp.int32, (size, krylov), 0) // ny
         == lax.broadcasted_iota(jnp.int32, (size, krylov), 1)
     ).astype(f32)
-    gram_send[...] = jnp.dot(kept, pick, precision=HIGHEST, preferred_element_type=f32)
+    gram = jnp.dot(kept, pick, precision=HIGHEST, preferred_element_type=f32)
+    blocks, height = gram_blocks(krylov, nz)
+    gram_send[...] = jnp.concatenate(
+        [gram[n * height : (n + 1) * height] for n in range(blocks)], axis=1
+    )
 
     pl.semaphore_wait(barrier, tiles - 1 + groups - 1)
 
@@ -289,7 +298,10 @@
     coef_send[...] = inner[0:1]
     coef_begin()
     gram_arrive()
-    gram = jnp.sum(gram_all[...], axis=0) / count
+    packed = jnp.sum(gram_all[...], axis=0) / count
+    gram = jnp.concatenate(
+        [packed[:, n * krylov : (n + 1) * krylov] for n in range(blocks)], axis=0
+    )
     coef_arrive()
     first_coef = jnp.sum(coef_all[...], axis=0) / count
     first_rows = jnp.broadcast_to(first_coef, (8, krylov))
@@ -349,6 +361,7 @@
     rim = 3 * steps
     planes = slab + 2 * rim
     count = len(spans(slab, rim))
+    blocks, height = gram_blocks(krylov, nz)
     dma = pltpu.SemaphoreType.DMA
     field = pltpu.VMEM((parts, planes, ny, nz), f32)
     whole = pl.BlockSpec(memory_space=pltpu.VMEM)
@@ -376,8 +389,8 @@
             pltpu.VMEM((krylov * ny, krylov * ny), f32),
             pltpu.VMEM((krylov, nz), f32),
             pltpu.VMEM((krylov, 8, nz), f32),
-            pltpu.VMEM((krylov, krylov), f32),
-            pltpu.VMEM((tiles, krylov, krylov), f32),
+            pltpu.VMEM((height, blocks * krylov), f32),
+            pltpu.VMEM((tiles, height, blocks * krylov), f32),
             pltpu.VMEM((1, krylov), f32),
             pltpu.VMEM((tiles, 1, krylov), f32),
             pltpu.VMEM((1, nz), f32),

time: 36.4 us -> 35.2 us (0.967)
  Pallas kernels: 35.5 us -> 34.3 us
    pallas_call x1, Pallas kernels: 33.9 us -> 32.7 us  [on_device(): pl.pallas_call(functools.partial(kernel, groups, tiles), name='propagate'...]
where the time goes in v3:
time: 35.2 us; the launch traced here: 35 us
  Pallas kernels  34.3 us (97%)
  between operations  0.64 us (2%)
    pallas_call x1, Pallas kernels, on_device(): pl.pallas_call(functools.partial(kernel, groups, tiles), name='propagate'...  32.7 us
    pallas_call x1, Pallas kernels, on_device(): pl.pallas_call(finish, name='finish', out_shape=tuple((jax.ShapeDtypeStru...  1.62 us

profile of v3, /device:TPU:0, one launch (start us, length us, event | category | flops | bytes accessed | tf_op | source)
XLA Modules:
  0.0 35.0 jit_solution(7282447391753266607)
XLA Ops:
  0.6 32.7 %propagate.1 = (f32[1,5,4,16,128]{4,3,2,1,0:T(8,128)}, f32[1,32]{1,0:T(1,128)}, f32[1,128]{1,0:T(1,128)}) custom-call(f32[5,5]{1,0:T(8,128)} %coupling.1, bf16[32,5,4,16,128]{4,3,2,1,0:T(8,128)(2,1)} %basis.1, bf16[1,4,4,16,128]{4,3,2,1,0:T(8,128)(2,1)} %snapshots.1), custom_call_target="tpu_custom_call" | custom-call | tf_op jit(solution)/shard_map/propagate/pallas_call | solution.py:368
  33.3 1.6 %finish.1 = (f32[1,5,4,16,128]{4,3,2,1,0:T(8,128)}, f32[1,32]{1,0:T(1,128)}, f32[1,128]{1,0:T(1,128)}) custom-call(f32[1,5,4,16,128]{4,3,2,1,0:T(8,128)} %get-tuple-element.9.left, f32[1,32]{1,0:T(1,128)} %get-tuple-element.10.coefs, f32[1,128]{1,0:T(1,128)} %get-tuple-element.11.square), custom_call_target="tpu_custom_call" | custom-call | tf_op jit(solution)/shard_map/finish/pallas_call | solution.py:414
